TPU v7x, 256 devices: a whole 4x4x8 slice. The times are simulated.
256 devices in a mesh: seq: 16 (over x, z_lo), ch: 16 (over z_hi, y, core).
Axes of the slice: x: 4, y: 4, z: 8 (z_hi: 2, z_lo: 4; z = z_hi * 4 + z_lo), core: 2. Of those that a mesh axis runs over, the one named last changes fastest.
Arguments:
- signal: bfloat16 [8192, 2048], P('seq', 'ch'), may hold values from -6 to 6
- filter_raw: bfloat16 [8192, 2048], P('seq', 'ch'), may hold values from -6 to 6
- gate: bfloat16 [8192, 2048], P('seq', 'ch'), may hold values from -6 to 6
- d_out: bfloat16 [8192, 2048], P('seq', 'ch'), may hold values from -6 to 6
- w_first: bfloat16 [32, 64, 64], P('ch'), may hold values from -0.75 to 0.75
- w_second: bfloat16 [64, 32, 32], P('ch'), may hold values from -1 to 1
Outputs:
- grad_signal: bfloat16 [8192, 2048], P('seq', 'ch')
- grad_filter: bfloat16 [8192, 2048], P('seq', 'ch')
- grad_gate: bfloat16 [8192, 2048], P('seq', 'ch')
- grad_first: float32 [32, 64, 64], P('ch', 'seq')
- grad_second: float32 [64, 32, 32], P('ch', 'seq')
All inputs are finite; a program needn't handle non-finite values.
Results may differ from a plain program's by a relative error of at most 0.02.
Values may be sent and summed in bfloat16 or wider, within the bound.
No kernel may reach another device: no remote copies, remote signals or barrier semaphores. Data moves between devices by JAX's collectives and lax.ppermute only.
A program may use at most 64 MiB of HBM per device.

v0:
```python
import math
import jax
import jax.numpy as jnp
from jax import lax
from jax.sharding import PartitionSpec as P

HIGHEST = lax.Precision.HIGHEST


def counting(count):
    return jnp.arange(count, dtype=jnp.int32)


def phase_table(row_ids, col_ids, length, sign):
    angles = (
        2.0 * math.pi / length * (row_ids[:, None] * col_ids[None, :] % length).astype(jnp.float32)
    )
    return (jnp.cos(angles), sign * jnp.sin(angles))


def contract(form, table, real_part, imag_part):
    cosine, sine = table
    out_real = jnp.einsum(form, cosine, real_part, precision=HIGHEST) - jnp.einsum(
        form, sine, imag_part, precision=HIGHEST
    )
    out_imag = jnp.einsum(form, cosine, imag_part, precision=HIGHEST) + jnp.einsum(
        form, sine, real_part, precision=HIGHEST
    )
    return (out_real, out_imag)


def rotate(cosine, sine, real_part, imag_part):
    return (real_part * cosine - imag_part * sine, real_part * sine + imag_part * cosine)


def factors(length):
    return (length // 128, 128)


def local_forward(real_part, imag_part):
    fields, group, rows, width = real_part.shape
    outer, inner = factors(rows)
    real_part = real_part.reshape(fields, group, outer, inner, width)
    imag_part = imag_part.reshape(fields, group, outer, inner, width)
    real_part, imag_part = contract(
        "qa,fkabc->fkqbc",
        phase_table(counting(outer), counting(outer), outer, -1.0),
        real_part,
        imag_part,
    )
    cosine, sine = phase_table(counting(outer), counting(inner), rows, -1.0)
    real_part, imag_part = rotate(cosine[:, :, None], sine[:, :, None], real_part, imag_part)
    return contract(
        "rb,fkqbc->fkqrc",
        phase_table(counting(inner), counting(inner), inner, -1.0),
        real_part,
        imag_part,
    )


def local_inverse(real_part, imag_part):
    fields, group, outer, inner, width = real_part.shape
    rows = outer * inner
    real_part, imag_part = contract(
        "br,fkqrc->fkqbc",
        phase_table(counting(inner), counting(inner), inner, 1.0),
        real_part,
        imag_part,
    )
    cosine, sine = phase_table(counting(outer), counting(inner), rows, 1.0)
    real_part, imag_part = rotate(cosine[:, :, None], sine[:, :, None], real_part, imag_part)
    real_part, imag_part = contract(
        "aq,fkqbc->fkabc",
        phase_table(counting(outer), counting(outer), outer, 1.0),
        real_part,
        imag_part,
    )
    return (
        real_part.reshape(fields, group, rows, width),
        imag_part.reshape(fields, group, rows, width),
    )


def forward_transform(fields):
    devices = lax.axis_size("seq")
    count, rows, width = fields.shape
    piece = rows // devices
    span = 2 * devices
    whole = span * rows
    parts = lax.all_to_all(fields[:, None], "seq", split_axis=2, concat_axis=1, tiled=True)
    cosine, sine = phase_table(counting(span), counting(devices), span, -1.0)
    real_part = jnp.einsum("ka,fabc->fkbc", cosine, parts, precision=HIGHEST)
    imag_part = jnp.einsum("ka,fabc->fkbc", sine, parts, precision=HIGHEST)
    positions = lax.axis_index("seq") * piece + counting(piece)
    cosine, sine = phase_table(counting(span), positions, whole, -1.0)
    real_part, imag_part = rotate(cosine[:, :, None], sine[:, :, None], real_part, imag_part)
    spectrum = lax.all_to_all(
        jnp.stack([real_part, imag_part], axis=1), "seq", split_axis=2, concat_axis=3, tiled=True
    )
    return local_forward(spectrum[:, 0], spectrum[:, 1])


def inverse_transform(real_part, imag_part):
    devices = lax.axis_size("seq")
    real_part, imag_part = local_inverse(real_part, imag_part)
    group = real_part.shape[1]
    rows = real_part.shape[2]
    span = 2 * devices
    whole = span * rows
    classes = lax.axis_index("seq") * group + counting(group)
    cosine, sine = phase_table(classes, counting(rows), whole, 1.0)
    real_part, imag_part = rotate(cosine[:, :, None], sine[:, :, None], real_part, imag_part)
    gathered = lax.all_to_all(
        jnp.stack([real_part, imag_part], axis=1), "seq", split_axis=3, concat_axis=2, tiled=True
    )
    cosine, sine = phase_table(counting(devices), counting(span), span, 1.0)
    inverse_scale = 1.0 / whole
    out_real = (
        jnp.einsum("ak,fkbc->fabc", cosine, gathered[:, 0], precision=HIGHEST)
        - jnp.einsum("ak,fkbc->fabc", sine, gathered[:, 1], precision=HIGHEST)
    ) * inverse_scale
    slab = lax.all_to_all(out_real, "seq", split_axis=1, concat_axis=2, tiled=True)
    return slab[:, 0]


def adjoint_spectra(spectra_real, spectra_imag, incoming_real, incoming_imag):
    toward_signal_real = spectra_real[1] * incoming_real + spectra_imag[1] * incoming_imag
    toward_signal_imag = spectra_real[1] * incoming_imag - spectra_imag[1] * incoming_real
    toward_filter_real = spectra_real[0] * incoming_real + spectra_imag[0] * incoming_imag
    toward_filter_imag = spectra_real[0] * incoming_imag - spectra_imag[0] * incoming_real
    return (toward_signal_real, toward_signal_imag, toward_filter_real, toward_filter_imag)


def shards(signal, filter_raw, gate, d_out, w_first, w_second):
    rows, width = signal.shape
    scale = float(rows * lax.axis_size("seq")) ** (-0.5)
    signal_wide = signal.astype(jnp.float32)
    kernel = filter_raw.astype(jnp.float32) * scale
    spectra_real, spectra_imag = forward_transform(jnp.stack([signal_wide, kernel]))
    mixed_real = spectra_real[0] * spectra_real[1] - spectra_imag[0] * spectra_imag[1]
    mixed_imag = spectra_real[0] * spectra_imag[1] + spectra_imag[0] * spectra_real[1]
    conv = inverse_transform(mixed_real[None], mixed_imag[None])[0].astype(jnp.bfloat16)
    gate_wide = gate.astype(jnp.float32)
    product = (conv.astype(jnp.float32) * gate_wide).astype(jnp.bfloat16)
    blocks = w_first.shape[0]
    block = w_first.shape[1]
    product_blocks = product.reshape(rows, blocks, block)
    first_mix = jnp.einsum(
        "tij,ijk->tik", product_blocks, w_first, preferred_element_type=jnp.float32
    ).astype(jnp.bfloat16)
    received = lax.all_to_all(first_mix, "ch", split_axis=2, concat_axis=1, tiled=True)
    incoming = d_out.reshape(rows, w_second.shape[0], w_second.shape[1])
    second_back = jnp.einsum(
        "tko,kio->tki", incoming, w_second, preferred_element_type=jnp.float32
    ).astype(jnp.bfloat16)
    grad_second = jnp.einsum("tik,tko->kio", received, incoming, preferred_element_type=jnp.float32)
    returned = lax.all_to_all(second_back, "ch", split_axis=2, concat_axis=1, tiled=True)
    grad_product = jnp.einsum(
        "tki,ijk->tij", returned, w_first, preferred_element_type=jnp.float32
    ).reshape(rows, width)
    grad_first = jnp.einsum(
        "tij,tki->ijk", product_blocks, returned, preferred_element_type=jnp.float32
    )
    grad_gate = (grad_product * conv.astype(jnp.float32)).astype(jnp.bfloat16)
    grad_conv = grad_product * gate_wide
    incoming_real, incoming_imag = forward_transform(grad_conv[None])
    sig_real, sig_imag, fil_real, fil_imag = adjoint_spectra(
        spectra_real, spectra_imag, incoming_real[0], incoming_imag[0]
    )
    results = inverse_transform(jnp.stack([sig_real, fil_real]), jnp.stack([sig_imag, fil_imag]))
    grad_signal = results[0].astype(jnp.bfloat16)
    grad_filter = (results[1] * scale).astype(jnp.bfloat16)
    grad_first = lax.psum_scatter(
        grad_first.astype(jnp.bfloat16), "seq", scatter_dimension=1, tiled=True
    ).astype(jnp.float32)
    grad_second = lax.psum_scatter(grad_second, "seq", scatter_dimension=1, tiled=True)
    return (grad_signal, grad_filter, grad_gate, grad_first, grad_second)


def solution(mesh):
    in_specs = (
        P("seq", "ch"),
        P("seq", "ch"),
        P("seq", "ch"),
        P("seq", "ch"),
        P("ch", None, None),
        P("ch", None, None),
    )
    out_specs = (
        P("seq", "ch"),
        P("seq", "ch"),
        P("seq", "ch"),
        P("ch", "seq", None),
        P("ch", "seq", None),
    )
    return jax.shard_map(shards, mesh=mesh, in_specs=in_specs, out_specs=out_specs, check_vma=False)
```

profile of v0, /device:TPU:8, one launch (start us, length us, event | category | flops | bytes accessed | tf_op | source)
XLA Modules:
  0.0 462.7 jit_solution(11425884564633815950)
XLA Ops:
  2.8 20.1 %all_to_all.147 = bf16[512,4,32]{0,1,2:T(4,128)(2,1)S(1)} all-to-all(bf16[512,4,32]{0,1,2:T(4,128)(2,1)S(1)} %copy.234), channel_id=1, replica_groups=mesh['seq'=16,'ch'=16] {'ch'}, dimensions={2} | all-to-all | bytes 262144 | tf_op jit(solution)/shard_map/all_to_all | solution.py:157
  24.1 5.8 %all-to-all-start.3 = ((f32[1,1,512,128]{3,1,0,2:T(1,128)}), f32[1,1,512,128]{3,1,0,2:T(1,128)S(1)}, u32[]{:S(2)}, u32[]{:S(2)}) async-start(f32[1,1,512,128]{3,1,0,2:T(1,128)} %bitcast.38), calls=%async_computation.3 | async-start | bytes 524288 | tf_op jit(solution)/shard_map/all_to_all | solution.py:90
  31.2 10.9 %all-to-all-done.3 = f32[1,1,512,128]{3,1,0,2:T(1,128)S(1)} async-done(((f32[1,1,512,128]{3,1,0,2:T(1,128)}), f32[1,1,512,128]{3,1,0,2:T(1,128)S(1)}, u32[]{:S(2)}, u32[]{:S(2)}) %all-to-all-start.3) | async-done | bytes 262176 | tf_op jit(solution)/shard_map/all_to_all | solution.py:90
  42.1 3.6 all-to-all-start
  49.2 13.6 %all-to-all-done = f32[2,1,512,128]{3,0,1,2:T(2,128)S(1)} async-done(((f32[2,1,512,128]{3,0,1,2:T(2,128)}), f32[2,1,512,128]{3,0,1,2:T(2,128)S(1)}, u32[]{:S(2)}, u32[]{:S(2)}) %all-to-all-start) | async-done | bytes 524320 | tf_op jit(solution)/shard_map/all_to_all | solution.py:90
  62.7 3.7 all-to-all-start.4
  69.5 2.6 copy.222
  72.1 21.8 %all-to-all-done.4 = f32[1,2,32,32,128]{4,3,1,0,2:T(8,128)S(1)} async-done(((f32[1,2,32,32,128]{4,3,1,0,2:T(8,128)}), f32[1,2,32,32,128]{4,3,1,0,2:T(8,128)S(1)}, u32[]{:S(2)}, u32[]{:S(2)}) %all-to-all-start.4) | async-done | bytes 1048608 | tf_op jit(solution)/shard_map/all_to_all | solution.py:97
  93.9 4.2 all-to-all-start.1
  103.5 2.7 add_bitcast_fusion.3
  112.7 35.0 %all-to-all-done.1 = f32[2,2,32,32,128]{4,3,0,1,2:T(8,128)S(1)} async-done(((f32[2,2,32,32,128]{4,3,0,1,2:T(8,128)}), f32[2,2,32,32,128]{4,3,0,1,2:T(8,128)S(1)}, u32[]{:S(2)}, u32[]{:S(2)}) %all-to-all-start.1) | async-done | bytes 2097184 | tf_op jit(solution)/shard_map/all_to_all | solution.py:97
  148.1 2.7 fusion.27
  150.8 2.5 fusion.23
  153.3 2.6 fusion.5
  156.0 4.9 %multiply_subtract_fusion = (f32[2,2,4,128,128]{4,2,3,1,0:T(4,128)}, f32[2,2,4,128,128]{4,2,3,1,0:T(4,128)S(1)}) fusion(f32[2,2,4,128,128]{4,2,3,1,0:T(4,128)S(1)} %fusion.5, f32[4,128]{0,1:T(8,128)S(1)} %copy.230, f32[4,128]{0,1:T(8,128)S(1)} %copy-done.11, f32[2,2,128,128,4]{3,4,2,1,0:T(4,128)S(1)} %fusion.23, f32[2,2,4,128,128]{4,3,2,1,0:T(8,128)S(1)} %bitcast.367), kind=kOutput, calls=%fused_computation.63 | convolution fusion | flops 14418160 | bytes 5246976 | tf_op jit(solution)/shard_map/qa,fkabc->fkqbc/dot_general | solution.py:26
  161.2 2.2 fusion.70
  168.7 1.9 multiply_subtract_fusion.2
  180.0 2.1 fusion.6
  185.4 4.5 all-to-all-start.7
  197.8 2.1 fusion
  201.9 2.2 fusion.1
  204.3 13.0 %all-to-all-done.7 = f32[1,2,2,512,128]{4,2,1,0,3:T(2,128)} async-done(((f32[1,2,2,512,128]{4,2,1,0,3:T(2,128)}), f32[1,2,2,512,128]{4,2,1,0,3:T(2,128)}, u32[]{:S(2)}, u32[]{:S(2)}) %all-to-all-start.7) | async-done | bytes 1048608 | tf_op jit(solution)/shard_map/all_to_all | solution.py:113
  221.0 4.2 all-to-all-start.8
  225.7 3.0 copy.261
  228.7 4.9 %all-to-all-done.8 = bf16[1,16,32,128]{3,2,0,1:T(8,128)(2,1)} async-done(((bf16[1,16,32,128]{3,2,0,1:T(8,128)(2,1)}), bf16[1,16,32,128]{3,2,0,1:T(8,128)(2,1)}, u32[]{:S(2)}, u32[]{:S(2)}) %all-to-all-start.8) | async-done | bytes 131104 | tf_op jit(solution)/shard_map/all_to_all | solution.py:122
  233.6 3.7 all-to-all-start.5
  240.1 45.9 %all-to-all-done.5 = f32[2,2,2,512,128]{4,2,0,1,3:T(2,128)S(1)} async-done(((f32[2,2,2,512,128]{4,2,0,1,3:T(2,128)}), f32[2,2,2,512,128]{4,2,0,1,3:T(2,128)S(1)}, u32[]{:S(2)}, u32[]{:S(2)}) %all-to-all-start.5) | async-done | bytes 2097184 | tf_op jit(solution)/shard_map/all_to_all | solution.py:113
  286.0 3.9 all-to-all-start.9
  294.4 4.3 all-to-all-done.9
  298.7 3.7 all-to-all-start.6
  304.5 80.4 %all-reduce = bf16[2,64,64]{2,1,0:T(8,128)(2,1)S(1)} all-reduce(bf16[2,64,64]{2,1,0:T(8,128)(2,1)S(1)} %convolution_convert_fusion.2), channel_id=2, replica_groups=mesh['seq'=16,'ch'=16] {'seq'}, use_global_device_ids=true, to_apply=%region_0.1.clone | all-reduce | flops 8192 | bytes 32768
  385.9 74.6 %all-reduce.1 = f32[4,32,32]{2,0,1:T(4,128)S(1)} all-reduce(f32[4,32,32]{2,0,1:T(4,128)S(1)} %copy.283), channel_id=3, replica_groups=mesh['seq'=16,'ch'=16] {'seq'}, use_global_device_ids=true, to_apply=%region_1.2.clone | all-reduce | flops 4096 | bytes 32768
  (132 shorter events, 66.5 us)
Async XLA Ops:
  0.6 22.4 %copy-start = (bf16[2,64,64]{2,1,0:T(8,128)(2,1)S(1)}, bf16[2,64,64]{2,1,0:T(8,128)(2,1)}, u32[]{:S(2)}) copy-start(bf16[2,64,64]{2,1,0:T(8,128)(2,1)} %param.10) | copy-start | bytes 49156
  0.6 22.7 %copy-start.12 = (bf16[512,128]{1,0:T(8,128)(2,1)S(1)}, bf16[512,128]{1,0:T(8,128)(2,1)}, u32[]{:S(2)}) copy-start(bf16[512,128]{1,0:T(8,128)(2,1)} %param.8) | copy-start | bytes 393220
  0.7 29.2 %copy-start.14 = (bf16[512,128]{1,0:T(8,128)(2,1)S(1)}, bf16[512,128]{1,0:T(8,128)(2,1)}, u32[]{:S(2)}) copy-start(bf16[512,128]{1,0:T(8,128)(2,1)} %param.6) | copy-start | bytes 393220
  0.7 29.2 %copy-start.15 = (bf16[512,128]{1,0:T(8,128)(2,1)S(1)}, bf16[512,128]{1,0:T(8,128)(2,1)}, u32[]{:S(2)}) copy-start(bf16[512,128]{1,0:T(8,128)(2,1)} %param.7) | copy-start | bytes 393220
  1.7 22.3 %copy-start.6 = (bf16[512,128]{0,1:T(8,128)(2,1)}, bf16[512,128]{0,1:T(8,128)(2,1)S(1)}, u32[]{:S(2)}) copy-start(bf16[512,128]{0,1:T(8,128)(2,1)S(1)} %copy.233) | copy-start | bytes 393220
  23.0 1.1 copy-start.8
  24.1 18.1 %all-to-all-start.3 = ((f32[1,1,512,128]{3,1,0,2:T(1,128)}), f32[1,1,512,128]{3,1,0,2:T(1,128)S(1)}, u32[]{:S(2)}, u32[]{:S(2)}) async-start(f32[1,1,512,128]{3,1,0,2:T(1,128)} %bitcast.38), calls=%async_computation.3 | async-start | bytes 524288 | tf_op jit(solution)/shard_map/all_to_all | solution.py:90
  42.1 20.6 %all-to-all-start = ((f32[2,1,512,128]{3,0,1,2:T(2,128)}), f32[2,1,512,128]{3,0,1,2:T(2,128)S(1)}, u32[]{:S(2)}, u32[]{:S(2)}) async-start(f32[2,1,512,128]{3,0,1,2:T(2,128)} %maximum_bitcast_fusion), calls=%async_computation | async-start | bytes 1048576 | tf_op jit(solution)/shard_map/all_to_all | solution.py:90
  62.7 31.1 %all-to-all-start.4 = ((f32[1,2,32,32,128]{4,3,1,0,2:T(8,128)}), f32[1,2,32,32,128]{4,3,1,0,2:T(8,128)S(1)}, u32[]{:S(2)}, u32[]{:S(2)}) async-start(f32[1,2,32,32,128]{4,3,1,0,2:T(8,128)} %copy.240), calls=%async_computation.4 | async-start | bytes 2097152 | tf_op jit(solution)/shard_map/all_to_all | solution.py:97
  93.9 53.9 %all-to-all-start.1 = ((f32[2,2,32,32,128]{4,3,0,1,2:T(8,128)}), f32[2,2,32,32,128]{4,3,0,1,2:T(8,128)S(1)}, u32[]{:S(2)}, u32[]{:S(2)}) async-start(f32[2,2,32,32,128]{4,3,0,1,2:T(8,128)} %copy.222), calls=%async_computation.1 | async-start | bytes 4194304 | tf_op jit(solution)/shard_map/all_to_all | solution.py:97
  99.4 4.0 copy-start.10
  153.3 2.7 copy-start.11
  164.9 1.2 copy-start.2
  167.4 1.3 copy-start.4
  167.5 1.3 copy-start.5
  175.0 3.2 copy-start.3
  185.4 5.7 %copy-start.1 = (f32[1,2,4,128,128]{3,4,2,1,0:T(8,128)S(1)}, f32[1,2,4,128,128]{3,4,2,1,0:T(8,128)}, u32[]{:S(2)}) copy-start(f32[1,2,4,128,128]{3,4,2,1,0:T(8,128)} %get-tuple-element.37) | copy-start | bytes 1572868
  185.4 31.9 %all-to-all-start.7 = ((f32[1,2,2,512,128]{4,2,1,0,3:T(2,128)}), f32[1,2,2,512,128]{4,2,1,0,3:T(2,128)}, u32[]{:S(2)}, u32[]{:S(2)}) async-start(f32[1,2,2,512,128]{4,2,1,0,3:T(2,128)} %copy.273), calls=%async_computation.7 | async-start | bytes 2097152 | tf_op jit(solution)/shard_map/all_to_all | solution.py:113
  221.0 12.6 %all-to-all-start.8 = ((bf16[1,16,32,128]{3,2,0,1:T(8,128)(2,1)}), bf16[1,16,32,128]{3,2,0,1:T(8,128)(2,1)}, u32[]{:S(2)}, u32[]{:S(2)}) async-start(bf16[1,16,32,128]{3,2,0,1:T(8,128)(2,1)} %copy.276), calls=%async_computation.8 | async-start | bytes 262144 | tf_op jit(solution)/shard_map/all_to_all | solution.py:122
  228.7 8.6 %copy-start.13 = (bf16[512,128]{1,0:T(8,128)(2,1)S(1)}, bf16[512,128]{1,0:T(8,128)(2,1)}, u32[]{:S(2)}) copy-start(bf16[512,128]{1,0:T(8,128)(2,1)} %param.8) | copy-start | bytes 393220
  233.6 52.4 %all-to-all-start.5 = ((f32[2,2,2,512,128]{4,2,0,1,3:T(2,128)}), f32[2,2,2,512,128]{4,2,0,1,3:T(2,128)S(1)}, u32[]{:S(2)}, u32[]{:S(2)}) async-start(f32[2,2,2,512,128]{4,2,0,1,3:T(2,128)} %copy.261), calls=%async_computation.5 | async-start | bytes 4194304 | tf_op jit(solution)/shard_map/all_to_all | solution.py:113
  286.0 12.7 %all-to-all-start.9 = ((bf16[512,2,64]{0,1,2:T(2,128)(2,1)}), bf16[512,2,64]{0,1,2:T(2,128)(2,1)S(1)}, u32[]{:S(2)}, u32[]{:S(2)}) async-start(bf16[512,2,64]{0,1,2:T(2,128)(2,1)} %copy.281), calls=%async_computation.9 | async-start | bytes 262144 | tf_op jit(solution)/shard_map/all_to_all | solution.py:151
  292.7 9.7 %copy-start.16 = (u32[256]{0:T(256)S(1)}, u32[256]{0:T(256)}, u32[]{:S(2)}) copy-start(u32[256]{0:T(256)} %constant.160) | copy-start | bytes 3076
  292.7 11.6 %copy-start.9 = (bf16[512,64,2]{0,1,2:T(8,128)(2,1)S(1)}, bf16[512,64,2]{0,1,2:T(8,128)(2,1)}, u32[]{:S(2)}) copy-start(bf16[512,64,2]{0,1,2:T(8,128)(2,1)} %copy-done.8) | copy-start | bytes 393220
  292.7 93.0 %copy-start.7 = (bf16[512,128]{0,1:T(8,128)(2,1)S(1)}, bf16[512,128]{0,1:T(8,128)(2,1)}, u32[]{:S(2)}) copy-start(bf16[512,128]{0,1:T(8,128)(2,1)} %copy-done.6) | copy-start | bytes 393220
  298.7 162.4 %all-to-all-start.6 = ((f32[2,16,32,128]{3,2,0,1:T(8,128)}), f32[2,16,32,128]{3,2,0,1:T(8,128)S(1)}, u32[]{:S(2)}, u32[]{:S(2)}) async-start(f32[2,16,32,128]{3,2,0,1:T(8,128)} %copy.264), calls=%async_computation.6 | async-start | bytes 1048576 | tf_op jit(solution)/shard_map/all_to_all | solution.py:122
where the time goes:
time: 470 us; the launch traced here: 463 us
  blocking collectives  175 us (37%)
  waiting for transfers between devices  149 us (32%)
  matrix products  63.8 us (14%)
  starting transfers between devices  37.1 us (8%)
  local copies, waits for them, and re-layouts  27.6 us (6%)
  other arithmetic  6.55 us (1%)
    unnamed x2, blocking collectives  155 us
    all_to_all x2, waiting for transfers between devices, inverse_transform(): lax.all_to_all(jnp.stack([real_part, imag_part], axis=1), 'seq', split_ax...  58.9 us
    all_to_all x2, waiting for transfers between devices, forward_transform(): lax.all_to_all(jnp.stack([real_part, imag_part], axis=1), 'seq', split_ax...  56.8 us
    all_to_all x2, waiting for transfers between devices, forward_transform(): lax.all_to_all(fields[:, None], 'seq', split_axis=2, concat_axis=1, tiled...  24.5 us
    all_to_all x1, blocking collectives, shards(): lax.all_to_all(second_back, 'ch', split_axis=2, concat_axis=1, tiled=True)  20.1 us
    dot_general x8, matrix products, contract(): jnp.einsum(form, sine, real_part, precision=HIGHEST)  15.6 us
    dot_general x8, matrix products, contract(): jnp.einsum(form, sine, imag_part, precision=HIGHEST)  14.7 us
    dot_general x8, matrix products, contract(): jnp.einsum(form, cosine, imag_part, precision=HIGHEST)  13.5 us
  transfers between devices with their start and end apart: 9, of which 8 were waited for; matrix products, arithmetic and copies ran while one was open for 11% of the time, Pallas kernels for 0%

commit v1 on v0

--- a/solution.py
+++ b/solution.py
@@ -154,7 +154,11 @@
         "tko,kio->tki", incoming, w_second, preferred_element_type=jnp.float32
     ).astype(jnp.bfloat16)
     grad_second = jnp.einsum("tik,tko->kio", received, incoming, preferred_element_type=jnp.float32)
-    returned = lax.all_to_all(second_back, "ch", split_axis=2, concat_axis=1, tiled=True)
+    _update_pieces_all = lambda load: jnp.concatenate(
+        lax.all_to_all(jnp.stack(jnp.split(load, lax.axis_size("ch"), axis=2), axis=0), "ch", 0, 0),
+        axis=1,
+    )
+    returned = _update_pieces_all(second_back)
     grad_product = jnp.einsum(
         "tki,ijk->tij", returned, w_first, preferred_element_type=jnp.float32
     ).reshape(rows, width)

time: 470 us -> 471 us (level)
  no operation moved by 1% of the time
where the time goes in v1:
time: 471 us; the launch traced here: 463 us
  blocking collectives  175 us (37%)
  waiting for transfers between devices  149 us (32%)
  matrix products  63.8 us (14%)
  starting transfers between devices  37.2 us (8%)
  local copies, waits for them, and re-layouts  28.2 us (6%)
  other arithmetic  6.55 us (1%)
    unnamed x2, blocking collectives  155 us
    all_to_all x2, waiting for transfers between devices, inverse_transform(): lax.all_to_all(jnp.stack([real_part, imag_part], axis=1), 'seq', split_ax...  58.9 us
    all_to_all x2, waiting for transfers between devices, forward_transform(): lax.all_to_all(jnp.stack([real_part, imag_part], axis=1), 'seq', split_ax...  56.8 us
    all_to_all x2, waiting for transfers between devices, forward_transform(): lax.all_to_all(fields[:, None], 'seq', split_axis=2, concat_axis=1, tiled...  24.5 us
    all_to_all x1, blocking collectives, shards(): lax.all_to_all(jnp.stack(jnp.split(load, lax.axis_size('ch'), axis=2), ax...  20.1 us
    dot_general x8, matrix products, contract(): jnp.einsum(form, sine, real_part, precision=HIGHEST)  15.6 us
    dot_general x8, matrix products, contract(): jnp.einsum(form, sine, imag_part, precision=HIGHEST)  14.7 us
    dot_general x8, matrix products, contract(): jnp.einsum(form, cosine, imag_part, precision=HIGHEST)  13.5 us
  transfers between devices with their start and end apart: 9, of which 8 were waited for; matrix products, arithmetic and copies ran while one was open for 11% of the time, Pallas kernels for 0%

profile of v1, /device:TPU:8, one launch (start us, length us, event | category | flops | bytes accessed | tf_op | source)
XLA Modules:
  0.0 463.3 jit_solution(17433466280358369679)
XLA Ops:
  3.0 20.1 %all_to_all.134 = bf16[16,512,4,2]{1,3,2,0:T(2,128)(2,1)S(1)} all-to-all(bf16[16,512,4,2]{1,3,2,0:T(2,128)(2,1)S(1)} %constant_dynamic-update-slice_fusion), channel_id=1, replica_groups=mesh['seq'=16,'ch'=16] {'ch'}, dimensions={0} | all-to-all | bytes 262144 | tf_op jit(solution)/shard_map/all_to_all | solution.py:158
  24.7 5.8 %all-to-all-start.3 = ((f32[1,1,512,128]{3,1,0,2:T(1,128)}), f32[1,1,512,128]{3,1,0,2:T(1,128)S(1)}, u32[]{:S(2)}, u32[]{:S(2)}) async-start(f32[1,1,512,128]{3,1,0,2:T(1,128)} %bitcast.54), calls=%async_computation.3 | async-start | bytes 524288 | tf_op jit(solution)/shard_map/all_to_all | solution.py:90
  31.8 10.9 %all-to-all-done.3 = f32[1,1,512,128]{3,1,0,2:T(1,128)S(1)} async-done(((f32[1,1,512,128]{3,1,0,2:T(1,128)}), f32[1,1,512,128]{3,1,0,2:T(1,128)S(1)}, u32[]{:S(2)}, u32[]{:S(2)}) %all-to-all-start.3) | async-done | bytes 262176 | tf_op jit(solution)/shard_map/all_to_all | solution.py:90
  42.7 3.6 all-to-all-start
  49.8 13.6 %all-to-all-done = f32[2,1,512,128]{3,0,1,2:T(2,128)S(1)} async-done(((f32[2,1,512,128]{3,0,1,2:T(2,128)}), f32[2,1,512,128]{3,0,1,2:T(2,128)S(1)}, u32[]{:S(2)}, u32[]{:S(2)}) %all-to-all-start) | async-done | bytes 524320 | tf_op jit(solution)/shard_map/all_to_all | solution.py:90
  63.3 3.7 all-to-all-start.4
  70.1 2.6 copy.224
  72.7 21.8 %all-to-all-done.4 = f32[1,2,32,32,128]{4,3,1,0,2:T(8,128)S(1)} async-done(((f32[1,2,32,32,128]{4,3,1,0,2:T(8,128)}), f32[1,2,32,32,128]{4,3,1,0,2:T(8,128)S(1)}, u32[]{:S(2)}, u32[]{:S(2)}) %all-to-all-start.4) | async-done | bytes 1048608 | tf_op jit(solution)/shard_map/all_to_all | solution.py:97
  94.5 4.2 all-to-all-start.1
  104.1 2.7 add_bitcast_fusion.3
  113.4 35.0 %all-to-all-done.1 = f32[2,2,32,32,128]{4,3,0,1,2:T(8,128)S(1)} async-done(((f32[2,2,32,32,128]{4,3,0,1,2:T(8,128)}), f32[2,2,32,32,128]{4,3,0,1,2:T(8,128)S(1)}, u32[]{:S(2)}, u32[]{:S(2)}) %all-to-all-start.1) | async-done | bytes 2097184 | tf_op jit(solution)/shard_map/all_to_all | solution.py:97
  148.7 2.7 fusion.27
  151.4 2.5 fusion.23
  153.9 2.6 fusion.5
  156.6 4.9 %multiply_subtract_fusion = (f32[2,2,4,128,128]{4,2,3,1,0:T(4,128)}, f32[2,2,4,128,128]{4,2,3,1,0:T(4,128)S(1)}) fusion(f32[2,2,4,128,128]{4,2,3,1,0:T(4,128)S(1)} %fusion.5, f32[4,128]{0,1:T(8,128)S(1)} %copy.232, f32[4,128]{0,1:T(8,128)S(1)} %copy-done.9, f32[2,2,128,128,4]{3,4,2,1,0:T(4,128)S(1)} %fusion.23, f32[2,2,4,128,128]{4,3,2,1,0:T(8,128)S(1)} %bitcast.426), kind=kOutput, calls=%fused_computation.63 | convolution fusion | flops 14418160 | bytes 5246976 | tf_op jit(solution)/shard_map/qa,fkabc->fkqbc/dot_general | solution.py:26
  161.8 2.2 fusion.73
  169.3 1.9 multiply_subtract_fusion.2
  180.6 2.1 fusion.6
  186.1 4.5 all-to-all-start.7
  198.4 2.1 fusion
  202.5 2.2 fusion.1
  204.9 13.0 %all-to-all-done.7 = f32[1,2,2,512,128]{4,2,1,0,3:T(2,128)} async-done(((f32[1,2,2,512,128]{4,2,1,0,3:T(2,128)}), f32[1,2,2,512,128]{4,2,1,0,3:T(2,128)}, u32[]{:S(2)}, u32[]{:S(2)}) %all-to-all-start.7) | async-done | bytes 1048608 | tf_op jit(solution)/shard_map/all_to_all | solution.py:113
  221.6 4.2 all-to-all-start.8
  226.3 3.0 copy.262
  229.3 4.9 %all-to-all-done.8 = bf16[1,16,32,128]{3,2,0,1:T(8,128)(2,1)} async-done(((bf16[1,16,32,128]{3,2,0,1:T(8,128)(2,1)}), bf16[1,16,32,128]{3,2,0,1:T(8,128)(2,1)}, u32[]{:S(2)}, u32[]{:S(2)}) %all-to-all-start.8) | async-done | bytes 131104 | tf_op jit(solution)/shard_map/all_to_all | solution.py:122
  234.2 3.7 all-to-all-start.5
  240.7 45.9 %all-to-all-done.5 = f32[2,2,2,512,128]{4,2,0,1,3:T(2,128)S(1)} async-done(((f32[2,2,2,512,128]{4,2,0,1,3:T(2,128)}), f32[2,2,2,512,128]{4,2,0,1,3:T(2,128)S(1)}, u32[]{:S(2)}, u32[]{:S(2)}) %all-to-all-start.5) | async-done | bytes 2097184 | tf_op jit(solution)/shard_map/all_to_all | solution.py:113
  286.6 3.9 all-to-all-start.9
  295.0 4.3 all-to-all-done.9
  299.3 3.7 all-to-all-start.6
  305.1 80.4 %all-reduce = bf16[2,64,64]{2,1,0:T(8,128)(2,1)S(1)} all-reduce(bf16[2,64,64]{2,1,0:T(8,128)(2,1)S(1)} %convolution_convert_fusion.2), channel_id=2, replica_groups=mesh['seq'=16,'ch'=16] {'seq'}, use_global_device_ids=true, to_apply=%region_0.1.clone | all-reduce | flops 8192 | bytes 32768
  386.5 74.6 %all-reduce.1 = f32[4,32,32]{2,0,1:T(4,128)S(1)} all-reduce(f32[4,32,32]{2,0,1:T(4,128)S(1)} %copy.285), channel_id=3, replica_groups=mesh['seq'=16,'ch'=16] {'seq'}, use_global_device_ids=true, to_apply=%region_1.2.clone | all-reduce | flops 4096 | bytes 32768
  (145 shorter events, 67.0 us)
Async XLA Ops:
  0.6 22.5 %copy-start = (bf16[2,64,64]{2,1,0:T(8,128)(2,1)S(1)}, bf16[2,64,64]{2,1,0:T(8,128)(2,1)}, u32[]{:S(2)}) copy-start(bf16[2,64,64]{2,1,0:T(8,128)(2,1)} %param.10) | copy-start | bytes 49156
  0.6 23.3 %copy-start.10 = (bf16[512,128]{1,0:T(8,128)(2,1)S(1)}, bf16[512,128]{1,0:T(8,128)(2,1)}, u32[]{:S(2)}) copy-start(bf16[512,128]{1,0:T(8,128)(2,1)} %param.8) | copy-start | bytes 393220
  0.7 29.8 %copy-start.14 = (bf16[512,128]{1,0:T(8,128)(2,1)S(1)}, bf16[512,128]{1,0:T(8,128)(2,1)}, u32[]{:S(2)}) copy-start(bf16[512,128]{1,0:T(8,128)(2,1)} %param.6) | copy-start | bytes 393220
  0.7 29.8 %copy-start.15 = (bf16[512,128]{1,0:T(8,128)(2,1)S(1)}, bf16[512,128]{1,0:T(8,128)(2,1)}, u32[]{:S(2)}) copy-start(bf16[512,128]{1,0:T(8,128)(2,1)} %param.7) | copy-start | bytes 393220
  1.7 22.9 %copy-start.6 = (bf16[512,128]{0,1:T(8,128)(2,1)}, bf16[512,128]{0,1:T(8,128)(2,1)S(1)}, u32[]{:S(2)}) copy-start(bf16[512,128]{0,1:T(8,128)(2,1)S(1)} %copy.235) | copy-start | bytes 393220
  23.1 0.7 copy-start.12
  24.7 18.1 %all-to-all-start.3 = ((f32[1,1,512,128]{3,1,0,2:T(1,128)}), f32[1,1,512,128]{3,1,0,2:T(1,128)S(1)}, u32[]{:S(2)}, u32[]{:S(2)}) async-start(f32[1,1,512,128]{3,1,0,2:T(1,128)} %bitcast.54), calls=%async_computation.3 | async-start | bytes 524288 | tf_op jit(solution)/shard_map/all_to_all | solution.py:90
  42.7 20.6 %all-to-all-start = ((f32[2,1,512,128]{3,0,1,2:T(2,128)}), f32[2,1,512,128]{3,0,1,2:T(2,128)S(1)}, u32[]{:S(2)}, u32[]{:S(2)}) async-start(f32[2,1,512,128]{3,0,1,2:T(2,128)} %maximum_bitcast_fusion), calls=%async_computation | async-start | bytes 1048576 | tf_op jit(solution)/shard_map/all_to_all | solution.py:90
  63.3 31.1 %all-to-all-start.4 = ((f32[1,2,32,32,128]{4,3,1,0,2:T(8,128)}), f32[1,2,32,32,128]{4,3,1,0,2:T(8,128)S(1)}, u32[]{:S(2)}, u32[]{:S(2)}) async-start(f32[1,2,32,32,128]{4,3,1,0,2:T(8,128)} %copy.241), calls=%async_computation.4 | async-start | bytes 2097152 | tf_op jit(solution)/shard_map/all_to_all | solution.py:97
  94.5 53.9 %all-to-all-start.1 = ((f32[2,2,32,32,128]{4,3,0,1,2:T(8,128)}), f32[2,2,32,32,128]{4,3,0,1,2:T(8,128)S(1)}, u32[]{:S(2)}, u32[]{:S(2)}) async-start(f32[2,2,32,32,128]{4,3,0,1,2:T(8,128)} %copy.224), calls=%async_computation.1 | async-start | bytes 4194304 | tf_op jit(solution)/shard_map/all_to_all | solution.py:97
  100.1 4.0 copy-start.8
  153.9 2.7 copy-start.9
  165.6 1.2 copy-start.2
  168.1 1.3 copy-start.4
  168.1 1.3 copy-start.5
  175.6 3.2 copy-start.3
  186.1 5.7 %copy-start.1 = (f32[1,2,4,128,128]{3,4,2,1,0:T(8,128)S(1)}, f32[1,2,4,128,128]{3,4,2,1,0:T(8,128)}, u32[]{:S(2)}) copy-start(f32[1,2,4,128,128]{3,4,2,1,0:T(8,128)} %get-tuple-element.37) | copy-start | bytes 1572868
  186.1 31.9 %all-to-all-start.7 = ((f32[1,2,2,512,128]{4,2,1,0,3:T(2,128)}), f32[1,2,2,512,128]{4,2,1,0,3:T(2,128)}, u32[]{:S(2)}, u32[]{:S(2)}) async-start(f32[1,2,2,512,128]{4,2,1,0,3:T(2,128)} %copy.274), calls=%async_computation.7 | async-start | bytes 2097152 | tf_op jit(solution)/shard_map/all_to_all | solution.py:113
  221.6 12.6 %all-to-all-start.8 = ((bf16[1,16,32,128]{3,2,0,1:T(8,128)(2,1)}), bf16[1,16,32,128]{3,2,0,1:T(8,128)(2,1)}, u32[]{:S(2)}, u32[]{:S(2)}) async-start(bf16[1,16,32,128]{3,2,0,1:T(8,128)(2,1)} %copy.277), calls=%async_computation.8 | async-start | bytes 262144 | tf_op jit(solution)/shard_map/all_to_all | solution.py:122
  229.3 8.6 %copy-start.11 = (bf16[512,128]{1,0:T(8,128)(2,1)S(1)}, bf16[512,128]{1,0:T(8,128)(2,1)}, u32[]{:S(2)}) copy-start(bf16[512,128]{1,0:T(8,128)(2,1)} %param.8) | copy-start | bytes 393220
  234.2 52.4 %all-to-all-start.5 = ((f32[2,2,2,512,128]{4,2,0,1,3:T(2,128)}), f32[2,2,2,512,128]{4,2,0,1,3:T(2,128)S(1)}, u32[]{:S(2)}, u32[]{:S(2)}) async-start(f32[2,2,2,512,128]{4,2,0,1,3:T(2,128)} %copy.262), calls=%async_computation.5 | async-start | bytes 4194304 | tf_op jit(solution)/shard_map/all_to_all | solution.py:113
  286.6 12.7 %all-to-all-start.9 = ((bf16[512,2,64]{0,1,2:T(2,128)(2,1)}), bf16[512,2,64]{0,1,2:T(2,128)(2,1)S(1)}, u32[]{:S(2)}, u32[]{:S(2)}) async-start(bf16[512,2,64]{0,1,2:T(2,128)(2,1)} %copy.283), calls=%async_computation.9 | async-start | bytes 262144 | tf_op jit(solution)/shard_map/all_to_all | solution.py:151
  293.3 9.7 %copy-start.16 = (u32[256]{0:T(256)S(1)}, u32[256]{0:T(256)}, u32[]{:S(2)}) copy-start(u32[256]{0:T(256)} %constant.160) | copy-start | bytes 3076
  293.3 11.6 %copy-start.13 = (bf16[16,512,4,2]{1,3,2,0:T(2,128)(2,1)S(1)}, bf16[16,512,4,2]{1,3,2,0:T(2,128)(2,1)}, u32[]{:S(2)}) copy-start(bf16[16,512,4,2]{1,3,2,0:T(2,128)(2,1)} %copy-done.12) | copy-start | bytes 393220
  293.3 93.0 %copy-start.7 = (bf16[512,128]{0,1:T(8,128)(2,1)S(1)}, bf16[512,128]{0,1:T(8,128)(2,1)}, u32[]{:S(2)}) copy-start(bf16[512,128]{0,1:T(8,128)(2,1)} %copy-done.6) | copy-start | bytes 393220
  299.3 162.4 %all-to-all-start.6 = ((f32[2,16,32,128]{3,2,0,1:T(8,128)}), f32[2,16,32,128]{3,2,0,1:T(8,128)S(1)}, u32[]{:S(2)}, u32[]{:S(2)}) async-start(f32[2,16,32,128]{3,2,0,1:T(8,128)} %copy.265), calls=%async_computation.6 | async-start | bytes 1048576 | tf_op jit(solution)/shard_map/all_to_all | solution.py:122
